TPU v7x, 512 devices: a whole 4x8x8 slice. The times are simulated.
512 devices in a mesh: group: 64 (over y_lo, z, core), tensor: 8 (over y_hi, x).
Axes of the slice: x: 4, y: 8 (y_hi: 2, y_lo: 4; y = y_hi * 4 + y_lo), z: 8, core: 2. Of those that a mesh axis runs over, the one named last changes fastest.
Arguments:
- turns: bfloat16 [64, 1024, 4096], P('group', 'tensor'), may hold values from -16 to 16
- query_store: bfloat16 [64, 64, 4096], P('group', None, 'tensor'), may hold values from -0.09375 to 0.09375
- key_block_holder: bfloat16 [64, 64, 4, 128], P('group'), may hold values from -0.09375 to 0.09375
- value_block_holder: bfloat16 [64, 64, 4, 128], P('group'), may hold values from -0.09375 to 0.09375
- query_bias: float32 [4096], P('tensor'), may hold values from -3 to 3
- key_projection_bias: float32 [512], replicated, may hold values from -3 to 3
- value_projection_bias: float32 [512], replicated, may hold values from -3 to 3
- owner: int32 [64], replicated, may hold values from 0 to 63, each once
- lengths: int32 [64], P('group'), may hold values from 1 to 1024, as said below
Outputs:
- attended: bfloat16 [64, 1024, 4096], P('group', None, 'tensor')
Inputs may be any that keep to these rules, and one draw needn't show every extreme that they name: `owner`: each group index holds exactly one block. `lengths`: some group's turn fills all 1024 positions.
All inputs are finite; a program needn't handle non-finite values.
Results may differ from a plain program's by a relative error of at most 0.0055.
The roundings to bfloat16 on the way count: a program that leaves them out, or rounds other values in their place, can miss the bound.
Values may be sent and summed in bfloat16 or wider, within the bound.
No kernel may reach another device: no remote copies, remote signals or barrier semaphores. Data moves between devices by JAX's collectives and lax.ppermute only.
A program may use at most 128 MiB of HBM per device.

v0:
```python
import jax
import jax.numpy as jnp
from jax import lax
from jax.sharding import PartitionSpec as P

QUERY_HEADS = 32
KEY_VALUE_HEADS = 4
HEAD_SIZE = 128
rotary_base = 1000000.0


def rotary(heads, positions):
    half = heads.shape[-1] // 2
    expo = jnp.arange(half, dtype=jnp.float32) * 2.0 / heads.shape[-1]
    freqs = rotary_base ** (-expo)
    angles = positions[:, None] * freqs[None, :]
    cosine = jnp.cos(angles)[None]
    sine = jnp.sin(angles)[None]
    first = heads[..., :half]
    second = heads[..., half:]
    return jnp.concatenate(
        [first * cosine - second * sine, second * cosine + first * sine], axis=-1
    )


def per_device(
    turns,
    query_store,
    key_block_holder,
    value_block_holder,
    query_bias,
    key_projection_bias,
    value_projection_bias,
    owner,
    lengths,
):
    tensor_index = lax.axis_index("tensor")
    group_count = lax.axis_size("group")
    gathered = lax.all_gather(turns, "tensor", axis=1, tiled=True)[0]
    token_count = gathered.shape[0]
    block_rows = query_store.shape[1]
    query_cols = query_store.shape[2]
    heads_dev = query_cols // HEAD_SIZE
    query_per_key_head = QUERY_HEADS // KEY_VALUE_HEADS
    key_value_per_group = max(1, heads_dev // query_per_key_head)
    key_value_leading = tensor_index * heads_dev // query_per_key_head
    keys_mine = lax.dynamic_slice_in_dim(
        key_block_holder, key_value_leading, key_value_per_group, 2
    ).reshape(1, block_rows, key_value_per_group * HEAD_SIZE)
    values_mine = lax.dynamic_slice_in_dim(
        value_block_holder, key_value_leading, key_value_per_group, 2
    ).reshape(1, block_rows, key_value_per_group * HEAD_SIZE)
    inverse = (
        jnp.zeros((group_count,), jnp.int32).at[owner].set(jnp.arange(group_count, dtype=jnp.int32))
    )
    ordered = jnp.take(gathered.reshape(token_count, group_count, block_rows), inverse, axis=1)
    proj_query = jnp.einsum(
        "tgc,gcn->tn",
        ordered,
        lax.all_gather(query_store, "group", axis=0, tiled=True),
        preferred_element_type=jnp.float32,
    )
    proj_key = jnp.einsum(
        "tgc,gcn->tn",
        ordered,
        lax.all_gather(keys_mine, "group", axis=0, tiled=True),
        preferred_element_type=jnp.float32,
    )
    proj_value = jnp.einsum(
        "tgc,gcn->tn",
        ordered,
        lax.all_gather(values_mine, "group", axis=0, tiled=True),
        preferred_element_type=jnp.float32,
    )
    key_bias_rows = lax.dynamic_slice_in_dim(
        key_projection_bias.reshape(KEY_VALUE_HEADS, HEAD_SIZE),
        key_value_leading,
        key_value_per_group,
        0,
    ).reshape(key_value_per_group * HEAD_SIZE)
    bias_values = lax.dynamic_slice_in_dim(
        value_projection_bias.reshape(KEY_VALUE_HEADS, HEAD_SIZE),
        key_value_leading,
        key_value_per_group,
        0,
    ).reshape(key_value_per_group * HEAD_SIZE)
    positions = jnp.arange(token_count, dtype=jnp.float32)
    raw_query = (
        (proj_query + query_bias).reshape(token_count, heads_dev, HEAD_SIZE).transpose(1, 0, 2)
    )
    unbiased_key = (
        (proj_key + key_bias_rows)
        .reshape(token_count, key_value_per_group, HEAD_SIZE)
        .transpose(1, 0, 2)
    )
    unbiased_value = (
        (proj_value + bias_values)
        .reshape(token_count, key_value_per_group, HEAD_SIZE)
        .transpose(1, 0, 2)
    )
    queries = rotary(raw_query, positions).astype(jnp.bfloat16)
    keys_rot = rotary(unbiased_key, positions).astype(jnp.bfloat16)
    values_cast = unbiased_value.astype(jnp.bfloat16)
    repeat_count = heads_dev // key_value_per_group
    keys_full = jnp.repeat(keys_rot, repeat_count, axis=0)
    values_full = jnp.repeat(values_cast, repeat_count, axis=0)
    index = jnp.arange(token_count, dtype=jnp.int32)
    span = min(256, token_count)
    outputs = []
    for block in range(token_count // span):
        first = block * span
        last = first + span
        scores = jnp.einsum(
            "htd,hsd->hts",
            queries[:, first:last],
            keys_full[:, :last],
            preferred_element_type=jnp.float32,
        ) * HEAD_SIZE ** (-0.5)
        causal = index[None, :last] <= index[first:last, None]
        scores = jnp.where(causal[None], scores, -jnp.inf)
        top = jnp.max(scores, axis=-1, keepdims=True)
        expd = jnp.exp(scores - top)
        weights = (expd / jnp.sum(expd, axis=-1, keepdims=True)).astype(jnp.bfloat16)
        outputs.append(
            jnp.einsum(
                "hts,hsd->htd", weights, values_full[:, :last], preferred_element_type=jnp.float32
            )
        )
    mixed = jnp.concatenate(outputs, axis=1)
    mixed = mixed.transpose(1, 0, 2).reshape(token_count, query_cols)
    live = (index < lengths[0])[:, None]
    return jnp.where(live, mixed, 0.0).astype(jnp.bfloat16)[None]


def solution(mesh):
    in_specs = (
        P("group", "tensor", None),
        P("group", None, "tensor"),
        P("group", None, None, None),
        P("group", None, None, None),
        P("tensor"),
        P(),
        P(),
        P(),
        P("group"),
    )
    out_specs = P("group", None, "tensor")
    return jax.shard_map(
        per_device, mesh=mesh, in_specs=in_specs, out_specs=out_specs, check_vma=False
    )
```

profile of v0, /device:TPU:57, one launch (start us, length us, event | category | flops | bytes accessed | tf_op | source)
XLA Modules:
  0.0 599.4 jit_solution(14467278969102455105)
XLA Ops:
  6.5 2.3 copy.34
  12.0 2.9 fusion.55
  18.9 167.7 %all-gather.7.cloned.1.call-done = bf16[1,1024,4096]{1,2,0:T(8,128)(2,1)} async-done(((bf16[1,128,4096]{1,2,0:T(8,128)(2,1)}), bf16[1,1024,4096]{1,2,0:T(8,128)(2,1)}) %all-gather.7.cloned.1.call-update) | async-done | bytes 8388624 | tf_op jit(solution)/shard_map/all_gather | solution.py:39
  186.7 8.9 %gather_fusion = bf16[64,1024,64]{1,2,0:T(8,128)(2,1)} fusion(bf16[1024,64,64]{0,2,1:T(8,128)(2,1)} %bitcast.67, s32[1024]{0:T(1024)S(1)} %pad_clamp_fusion), kind=kCustom, calls=%fused_computation | custom fusion | bytes 16777472 | tf_op jit(solution)/shard_map/jit(_take)/gather | solution.py:56
  195.6 122.6 %all-gather.11.cloned.1.call-done = bf16[64,64,1,128]{3,1,2,0:T(8,128)(2,1)} async-done(((bf16[1,64,1,128]{3,1,2,0:T(8,128)(2,1)}), bf16[64,64,1,128]{3,1,2,0:T(8,128)(2,1)}) %all-gather.11.cloned.1.call-update) | async-done | bytes 1048592 | tf_op jit(solution)/shard_map/all_gather | solution.py:66
  318.2 5.0 fusion.36
  323.3 1.2 fusion.84
  325.2 112.7 %all-gather.9.cloned.1.call-done = bf16[64,64,512]{2,1,0:T(8,128)(2,1)} async-done(((bf16[1,64,512]{2,1,0:T(8,128)(2,1)}), bf16[64,64,512]{2,1,0:T(8,128)(2,1)}) %all-gather.9.cloned.1.call-update) | async-done | bytes 4194320 | tf_op jit(solution)/shard_map/all_gather | solution.py:60
  437.9 10.5 %bitcast_add_fusion = f32[1024,512]{0,1:T(8,128)} fusion(bf16[64,64,512]{2,1,0:T(8,128)(2,1)} %all-gather.9.cloned.1.call-done, f32[512]{0:T(512)S(1)} %copy-done.9, bf16[64,1024,64]{1,2,0:T(8,128)(2,1)} %gather_fusion, pred[64]{0:T(512)(128)(4,1)S(1)} %compare_and_fusion), kind=kOutput, calls=%fused_computation.24 | convolution fusion | flops 4299685888 | bytes 14682176 | tf_op jit(solution)/shard_map/tgc,gcn->tn/dot_general | solution.py:57
  448.3 2.1 copy.35
  451.1 2.9 subtract_convert_fusion
  454.0 1.6 fusion.138
  455.6 1.2 fusion.26
  456.9 98.5 %all-gather.13.cloned.1.call-done = bf16[64,64,1,128]{3,1,2,0:T(8,128)(2,1)} async-done(((bf16[1,64,1,128]{3,1,2,0:T(8,128)(2,1)}), bf16[64,64,1,128]{3,1,2,0:T(8,128)(2,1)}) %all-gather.13.cloned.1.call-update) | async-done | bytes 1048592 | tf_op jit(solution)/shard_map/all_gather | solution.py:72
  555.3 6.4 %fusion.42 = bf16[1024,128]{1,0:T(8,128)(2,1)S(1)} fusion(bf16[64,64,1,128]{3,1,2,0:T(8,128)(2,1)} %all-gather.13.cloned.1.call-done, f32[128]{0:T(128)S(1)} %get-tuple-element.16, bf16[64,1024,64]{1,2,0:T(8,128)(2,1)} %gather_fusion, pred[64]{0:T(512)(128)(4,1)S(1)} %compare_and_fusion), kind=kOutput, calls=%fused_computation.48 | convolution fusion | flops 1078198272 | bytes 9699904 | tf_op jit(solution)/shard_map/tgc,gcn->tn/dot_general | solution.py:69
  563.3 1.7 copy.40
  566.0 2.3 fusion.58
  569.5 2.7 fusion.52
  572.2 2.0 fusion.133
  574.2 3.6 fusion.50
  577.8 6.1 %fusion.132 = (f32[4,256]{1,0:T(4,128)S(1)}, f32[4,256,768]{2,1,0:T(8,128)}) fusion(f32[4,256,768]{2,1,0:T(8,128)} %fusion.58, pred[256,768]{1,0:T(8,128)(4,1)} %broadcast_compare_fusion), kind=kOutput, calls=%fused_computation.136 | output fusion | flops 4719359 | bytes 6492160 | tf_op jit(solution)/shard_map/sub | solution.py:122
  584.0 2.0 fusion.131
  588.1 2.6 fusion.23
  591.6 1.3 copy.44
  (74 shorter events, 14.4 us)
Async XLA Ops:
  6.5 2.4 copy-start
  6.5 3.9 copy-start.8
  6.5 4.6 copy-start.10
  6.5 180.1 %all-gather.7.cloned.1.call-start = ((), (), s32[]{:S(2)}) async-start(), calls=%async_computation | async-start | bytes 9437184 | tf_op jit(solution)/shard_map/all_gather | solution.py:39
  8.9 309.4 %all-gather.11.cloned.1.call-start = ((), (), s32[]{:S(2)}) async-start(), calls=%async_computation.2 | async-start | bytes 1064960 | tf_op jit(solution)/shard_map/all_gather | solution.py:66
  9.6 428.3 %all-gather.9.cloned.1.call-start = ((), (), s32[]{:S(2)}) async-start(), calls=%async_computation.1 | async-start | bytes 4259840 | tf_op jit(solution)/shard_map/all_gather | solution.py:60
  10.4 545.0 %all-gather.13.cloned.1.call-start = ((), (), s32[]{:S(2)}) async-start(), calls=%async_computation.3 | async-start | bytes 1064960 | tf_op jit(solution)/shard_map/all_gather | solution.py:72
  318.2 119.7 %copy-start.9 = (f32[512]{0:T(512)S(1)}, f32[512]{0:T(512)}, u32[]{:S(2)}) copy-start(f32[512]{0:T(512)} %param.13) | copy-start | bytes 6148
  454.0 1.6 copy-start.1
  561.8 0.8 copy-start.3
  572.2 2.0 slice-start.1
  572.2 2.0 copy-start.7
  577.8 6.1 %copy-start.2 = (f32[4,256,1024]{2,1,0:T(8,128)S(1)}, f32[4,256,1024]{2,1,0:T(8,128)}, u32[]{:S(2)}) copy-start(f32[4,256,1024]{2,1,0:T(8,128)} %fusion.52) | copy-start | bytes 12582916
  577.8 6.1 %copy-start.5 = (pred[256,1024]{1,0:T(8,128)(4,1)S(1)}, pred[256,1024]{1,0:T(8,128)(4,1)}, u32[]{:S(2)}) copy-start(pred[256,1024]{1,0:T(8,128)(4,1)} %iota_compare_fusion) | copy-start | bytes 786436
  584.0 2.1 copy-start.4
  586.0 1.1 slice-start
  587.1 0.9 slice-start.2
  588.1 2.6 copy-start.6
Sparse Core Ops, SparseCore 0:
  10.4 176.2 all-gather.6
  188.8 129.3 all-gather.10
  320.4 117.4 all-gather.8
  439.9 115.4 all-gather.12
where the time goes:
time: 600 us; the launch traced here: 599 us
  waiting for transfers between devices  502 us (84%)
  matrix products  39.6 us (7%)
  local copies, waits for them, and re-layouts  23.1 us (4%)
  other arithmetic  20.3 us (3%)
  between operations  14.1 us (2%)
    all_gather x1, waiting for transfers between devices, per_device(): gathered = lax.all_gather(turns, 'tensor', axis=1, tiled=True)[0]  168 us
    all_gather x1, waiting for transfers between devices, per_device(): lax.all_gather(keys_mine, 'group', axis=0, tiled=True)  123 us
    all_gather x1, waiting for transfers between devices, per_device(): lax.all_gather(query_store, 'group', axis=0, tiled=True)  113 us
    all_gather x1, waiting for transfers between devices, per_device(): lax.all_gather(values_mine, 'group', axis=0, tiled=True)  98.5 us
  transfers between devices with their start and end apart: 4, of which 4 were waited for; matrix products, arithmetic and copies ran while one was open for 7% of the time, Pallas kernels for 0%

commit v1 on v0

--- a/solution.py
+++ b/solution.py
@@ -69,7 +69,9 @@
     proj_value = jnp.einsum(
         "tgc,gcn->tn",
         ordered,
-        lax.all_gather(values_mine, "group", axis=0, tiled=True),
+        jnp.concatenate(
+            lax.all_to_all(jnp.stack([values_mine] * lax.axis_size("group")), "group", 0, 0), axis=0
+        ),
         preferred_element_type=jnp.float32,
     )
     key_bias_rows = lax.dynamic_slice_in_dim(

time: 600 us -> 513 us (0.85)
  waiting for transfers between devices: 502 us -> 399 us
  starting transfers between devices: 0.12 us -> 14.9 us
    all_gather x1 -> x0, waiting for transfers between devices: 98.5 us -> none  [per_device(): lax.all_gather(values_mine, 'group', axis=0, tiled=True)]
    all_to_all x0 -> x1, starting transfers between devices: none -> 14.8 us  [per_device(): lax.all_to_all(jnp.stack([values_mine] * lax.axis_size('group')), 'group'...]
  transfers between devices with their start and end apart: 4 -> 4, of which waited for: 4 -> 3; matrix products, arithmetic and copies ran while one was open for 7% -> 9% of each run, Pallas kernels for 0% -> 0%
where the time goes in v1:
time: 513 us; the launch traced here: 512 us
  waiting for transfers between devices  399 us (78%)
  matrix products  39.6 us (8%)
  local copies, waits for them, and re-layouts  24.4 us (5%)
  other arithmetic  20.4 us (4%)
  starting transfers between devices  14.9 us (3%)
  between operations  14.1 us (3%)
    all_gather x1, waiting for transfers between devices, per_device(): gathered = lax.all_gather(turns, 'tensor', axis=1, tiled=True)[0]  163 us
    all_gather x1, waiting for transfers between devices, per_device(): lax.all_gather(keys_mine, 'group', axis=0, tiled=True)  123 us
    all_gather x1, waiting for transfers between devices, per_device(): lax.all_gather(query_store, 'group', axis=0, tiled=True)  113 us
    all_to_all x1, starting transfers between devices, per_device(): lax.all_to_all(jnp.stack([values_mine] * lax.axis_size('group')), 'group'...  14.8 us
    dot_general x1, matrix products, per_device(): jnp.einsum('tgc,gcn->tn', ordered, lax.all_gather(query_store, 'group', a...  10.5 us
  transfers between devices with their start and end apart: 4, of which 3 were waited for; matrix products, arithmetic and copies ran while one was open for 9% of the time, Pallas kernels for 0%

profile of v1, /device:TPU:57, one launch (start us, length us, event | category | flops | bytes accessed | tf_op | source)
XLA Modules:
  0.0 512.1 jit_solution(10293755158632685279)
XLA Ops:
  6.5 2.3 copy.33
  10.4 1.3 stack.3
  11.7 14.8 %all-to-all-start = ((bf16[64,1,64,128]{3,2,1,0:T(8,128)(2,1)}), bf16[64,1,64,128]{3,2,1,0:T(8,128)(2,1)}, u32[]{:S(2)}, u32[]{:S(2)}) async-start(bf16[64,1,64,128]{3,2,1,0:T(8,128)(2,1)} %stack.3), calls=%async_computation | async-start | bytes 2097152 | tf_op jit(solution)/shard_map/all_to_all | solution.py:73
  32.2 2.8 fusion.55
  35.1 162.6 %all-gather.5.cloned.1.call-done = bf16[1,1024,4096]{1,2,0:T(8,128)(2,1)} async-done(((bf16[1,128,4096]{1,2,0:T(8,128)(2,1)}), bf16[1,1024,4096]{1,2,0:T(8,128)(2,1)}) %all-gather.5.cloned.1.call-update) | async-done | bytes 8388624 | tf_op jit(solution)/shard_map/all_gather | solution.py:39
  197.7 8.9 %gather_fusion = bf16[64,1024,64]{1,2,0:T(8,128)(2,1)} fusion(bf16[1024,64,64]{0,2,1:T(8,128)(2,1)} %bitcast.70, s32[1024]{0:T(1024)S(1)} %pad_clamp_fusion), kind=kCustom, calls=%fused_computation | custom fusion | bytes 16777472 | tf_op jit(solution)/shard_map/jit(_take)/gather | solution.py:56
  206.6 122.7 %all-gather.9.cloned.1.call-done = bf16[64,64,1,128]{3,1,2,0:T(8,128)(2,1)} async-done(((bf16[1,64,1,128]{3,1,2,0:T(8,128)(2,1)}), bf16[64,64,1,128]{3,1,2,0:T(8,128)(2,1)}) %all-gather.9.cloned.1.call-update) | async-done | bytes 1048592 | tf_op jit(solution)/shard_map/all_gather | solution.py:66
  329.3 5.0 fusion.36
  336.2 112.7 %all-gather.7.cloned.1.call-done = bf16[64,64,512]{2,1,0:T(8,128)(2,1)} async-done(((bf16[1,64,512]{2,1,0:T(8,128)(2,1)}), bf16[64,64,512]{2,1,0:T(8,128)(2,1)}) %all-gather.7.cloned.1.call-update) | async-done | bytes 4194320 | tf_op jit(solution)/shard_map/all_gather | solution.py:60
  448.9 10.5 %bitcast_add_fusion = f32[1024,512]{0,1:T(8,128)} fusion(bf16[64,64,512]{2,1,0:T(8,128)(2,1)} %all-gather.7.cloned.1.call-done, f32[512]{0:T(512)S(1)} %copy-done.9, bf16[64,1024,64]{1,2,0:T(8,128)(2,1)} %gather_fusion, pred[64]{0:T(512)(128)(4,1)S(1)} %compare_and_fusion), kind=kOutput, calls=%fused_computation.24 | convolution fusion | flops 4299685888 | bytes 14682176 | tf_op jit(solution)/shard_map/tgc,gcn->tn/dot_general | solution.py:57
  459.4 2.1 copy.34
  462.1 2.9 subtract_convert_fusion
  465.1 1.6 fusion.138
  466.7 1.2 fusion.26
  467.9 6.4 %fusion.42 = bf16[1024,128]{1,0:T(8,128)(2,1)S(1)} fusion(bf16[64,1,64,128]{3,2,1,0:T(8,128)(2,1)} %all-to-all-done, f32[128]{0:T(128)S(1)} %fusion.111, bf16[64,1024,64]{1,2,0:T(8,128)(2,1)} %gather_fusion, pred[64]{0:T(512)(128)(4,1)S(1)} %compare_and_fusion), kind=kOutput, calls=%fused_computation.48 | convolution fusion | flops 1078198272 | bytes 9699904 | tf_op jit(solution)/shard_map/tgc,gcn->tn/dot_general | solution.py:69
  475.9 1.7 copy.39
  478.6 2.3 fusion.58
  482.1 2.7 fusion.52
  484.8 2.0 fusion.133
  486.8 3.6 fusion.50
  490.5 6.1 %fusion.132 = (f32[4,256]{1,0:T(4,128)S(1)}, f32[4,256,768]{2,1,0:T(8,128)}) fusion(f32[4,256,768]{2,1,0:T(8,128)} %fusion.58, pred[256,768]{1,0:T(8,128)(4,1)} %broadcast_compare_fusion), kind=kOutput, calls=%fused_computation.137 | output fusion | flops 4719359 | bytes 6492160 | tf_op jit(solution)/shard_map/sub | solution.py:124
  496.6 2.0 fusion.131
  500.7 2.6 fusion.23
  504.2 1.3 copy.43
  (75 shorter events, 15.7 us)
Async XLA Ops:
  6.5 2.4 copy-start
  6.5 3.8 copy-start.8
  6.5 20.7 %copy-start.10 = (s32[64]{0:T(128)S(1)}, s32[64]{0:T(128)}, u32[]{:S(2)}) copy-start(s32[64]{0:T(128)} %param.16) | copy-start | bytes 772
  6.5 191.1 %all-gather.5.cloned.1.call-start = ((), (), s32[]{:S(2)}) async-start(), calls=%async_computation.1 | async-start | bytes 9437184 | tf_op jit(solution)/shard_map/all_gather | solution.py:39
  8.9 320.4 %all-gather.9.cloned.1.call-start = ((), (), s32[]{:S(2)}) async-start(), calls=%async_computation.3 | async-start | bytes 1064960 | tf_op jit(solution)/shard_map/all_gather | solution.py:66
  9.6 439.3 %all-gather.7.cloned.1.call-start = ((), (), s32[]{:S(2)}) async-start(), calls=%async_computation.2 | async-start | bytes 4259840 | tf_op jit(solution)/shard_map/all_gather | solution.py:60
  11.7 456.2 %all-to-all-start = ((bf16[64,1,64,128]{3,2,1,0:T(8,128)(2,1)}), bf16[64,1,64,128]{3,2,1,0:T(8,128)(2,1)}, u32[]{:S(2)}, u32[]{:S(2)}) async-start(bf16[64,1,64,128]{3,2,1,0:T(8,128)(2,1)} %stack.3), calls=%async_computation | async-start | bytes 2097152 | tf_op jit(solution)/shard_map/all_to_all | solution.py:73
  206.6 242.3 %copy-start.9 = (f32[512]{0:T(512)S(1)}, f32[512]{0:T(512)}, u32[]{:S(2)}) copy-start(f32[512]{0:T(512)} %param.13) | copy-start | bytes 6148
  465.1 1.6 copy-start.1
  474.4 0.8 copy-start.3
  484.8 2.0 slice-start.1
  484.8 2.0 copy-start.7
  490.5 6.1 %copy-start.2 = (f32[4,256,1024]{2,1,0:T(8,128)S(1)}, f32[4,256,1024]{2,1,0:T(8,128)}, u32[]{:S(2)}) copy-start(f32[4,256,1024]{2,1,0:T(8,128)} %fusion.52) | copy-start | bytes 12582916
  490.5 6.1 %copy-start.5 = (pred[256,1024]{1,0:T(8,128)(4,1)S(1)}, pred[256,1024]{1,0:T(8,128)(4,1)}, u32[]{:S(2)}) copy-start(pred[256,1024]{1,0:T(8,128)(4,1)} %iota_compare_fusion) | copy-start | bytes 786436
  496.6 2.1 copy-start.4
  498.7 1.1 slice-start
  499.8 0.9 slice-start.2
  500.7 2.6 copy-start.6
Sparse Core Ops, SparseCore 0:
  10.4 187.2 all-gather.4
  199.8 129.3 all-gather.8
  331.4 117.4 all-gather.6
